TPU v7x, 32 devices: a whole 2x2x4 slice. The times are simulated.
32 devices in a mesh: groups: 2 (over y), seq: 4 (over z), dp: 4 (over x, core).
Axes of the slice: x: 2, y: 2, z: 4, core: 2. Of those that a mesh axis runs over, the one named last changes fastest.
Arguments:
- scan_input: bfloat16 [8, 512, 2048], P(('groups', 'dp'), 'seq'), parts along dimension 0, may hold values from -6 to 6
- gate_input: bfloat16 [8, 512, 2048], P(('groups', 'dp'), 'seq'), parts along dimension 0, may hold values from -6 to 6
- bmat: bfloat16 [8, 512, 128], P(('groups', 'dp'), 'seq'), parts along dimension 0, may hold values from -6 to 6
- cmat: bfloat16 [8, 512, 128], P(('groups', 'dp'), 'seq'), parts along dimension 0, may hold values from -0.5 to 0.5
- dt_raw: float32 [8, 512, 64], P(('groups', 'dp'), 'seq'), parts along dimension 0, may hold values from -4 to 4
- a_log: float32 [64], replicated
- d_skip: float32 [64], replicated, may hold values from 0.5 to 1.5
- gain: float32 [2048], replicated, may hold values from 0.1 to 1.9
- spans: int32 [8, 8, 2], P(('groups', 'dp')), parts along dimension 0, may hold values from 0 to 512, as said below
- cot: bfloat16 [8, 512, 2048], P(('groups', 'dp'), 'seq'), parts along dimension 0, may hold values from -6 to 6
Outputs:
- grad_x: bfloat16 [8, 512, 2048], P(('groups', 'dp'), 'seq'), parts along dimension 0
- grad_b: bfloat16 [8, 512, 128], P(('groups', 'dp'), 'seq'), parts along dimension 0
- grad_c: bfloat16 [8, 512, 128], P(('groups', 'dp'), 'seq'), parts along dimension 0
- grad_dt: float32 [8, 512, 64], P(('groups', 'dp'), 'seq'), parts along dimension 0
- grad_alog: float32 [128], P('groups'), parts along dimension 0
- grad_skip: float32 [128], P('groups'), parts along dimension 0
- grad_gain: float32 [4096], P('groups'), parts along dimension 0
There are 2 independent parts, one for each index of `groups`. A program takes and returns all parts, laid end to end along the dimension named above; an argument that names none is the same for every part. Nothing has to cross between parts.
Inputs may be any that keep to these rules, and one draw needn't show every extreme that they name: For each sequence the 8 spans are in order and tile the positions: the first starts at 0, each ends (exclusive) where the next starts, the last ends at 512, none is empty.
All inputs are finite; a program needn't handle non-finite values.
Results may differ from a plain program's by a relative error of at most 0.001.
Values sent between devices are 32-bit elements; how exact they have to be, the bound alone decides.
A program may use at most 128 MiB of HBM per device.

v0:
```python
import jax
import jax.numpy as jnp
from jax import lax
from jax.sharding import PartitionSpec as P

EPS = 1e-05
HI = lax.Precision.HIGHEST


def entering(shard, axis, combine, identity, reverse):
    peers, position = (lax.axis_size(axis), lax.axis_index(axis))
    everything = jax.tree.map(lambda part: lax.all_gather(part, axis), shard)
    start = jax.tree.map(
        lambda part, zero: jnp.broadcast_to(jnp.asarray(zero, part.dtype), part.shape),
        shard,
        identity,
    )

    def step(k, before):
        at = peers - 1 - k if reverse else k
        reached = at > position if reverse else at < position
        new = combine(before, jax.tree.map(lambda part: part[at], everything))
        return jax.tree.map(lambda a, b: jnp.where(reached, a, b), new, before)

    return lax.fori_loop(0, peers, step, start)


def combine(earlier, later):
    return (earlier[0] * later[0], later[0][:, None, None] * earlier[1] + later[1])


def on_device(scan_input, gate_input, bmat, cmat, dt_raw, a_log, d_skip, gain, spans, cot):
    rows = scan_input.shape[1]
    width = scan_input.shape[2]
    heads = a_log.shape[0]
    hdim = width // heads
    offset = lax.axis_index("seq") * rows
    xs = scan_input[0].astype(jnp.float32).reshape(rows, heads, hdim)
    zs = gate_input[0].astype(jnp.float32)
    bs = bmat[0].astype(jnp.float32)
    cs = cmat[0].astype(jnp.float32)
    raw = dt_raw[0]
    where_at = offset + jnp.arange(rows)
    flags = jnp.any(where_at[:, None] == spans[0][None, :, 0], 1).astype(jnp.int32)
    segl = jnp.cumsum(flags)
    step_size = jax.nn.softplus(raw)
    rate = jnp.exp(a_log)
    la = -rate[None, :] * step_size
    cum = jnp.cumsum(la, 0)
    place = jnp.arange(rows)
    same = (place[:, None] >= place[None, :]) & (segl[:, None] == segl[None, :])
    lmat = jnp.exp(jnp.where(same[None], cum.T[:, :, None] - cum.T[:, None, :], -jnp.inf))
    gmat = jnp.dot(cs, bs.T, precision=HI)
    xdt = xs * step_size[:, :, None]
    win = jnp.where((segl == 0)[:, None], jnp.exp(cum), 0.0)
    wout = jnp.exp(jnp.where((segl == segl[-1])[:, None], cum[-1][None, :] - cum, -jnp.inf))
    ablk = jnp.where(segl[-1] == 0, jnp.exp(cum[-1]), 0.0)
    weighted = xdt * wout[:, :, None]
    hloc = jnp.einsum("jhp,jn->hpn", weighted, bs, precision=HI)
    empty = jnp.zeros_like(hloc)
    _, hin = entering((ablk, hloc), "seq", combine, (jnp.ones_like(ablk), empty), False)
    sweights = lmat * gmat[None]
    y_intra = jnp.einsum("hij,jhp->ihp", sweights, xdt, precision=HI)
    cproj = jnp.einsum("in,hpn->ihp", cs, hin, precision=HI)
    y = y_intra + win[:, :, None] * cproj + d_skip[None, :, None] * xs
    gate = jax.nn.silu(zs)
    gated = y.reshape(rows, width) * gate
    scale = lax.rsqrt(jnp.mean(gated * gated, 1, keepdims=True) + EPS)
    normed = gated * scale
    upstream = cot[0].astype(jnp.float32)
    part_gain = jnp.sum(upstream * normed, 0)
    dnorm = upstream * gain[None, :]
    dgated = scale * dnorm - normed * scale * jnp.mean(dnorm * normed, 1, keepdims=True)
    dy = (dgated * gate).reshape(rows, heads, hdim)
    part_skip = jnp.sum(dy * xs, (0, 2))
    grad_in = dy * d_skip[None, :, None]
    dxdt = jnp.einsum("hij,ihp->jhp", sweights, dy, precision=HI)
    dsw = jnp.einsum("ihp,jhp->hij", dy, xdt, precision=HI)
    dgm = jnp.sum(dsw * lmat, 0)
    qmat = dsw * sweights
    dcum = jnp.sum(qmat, 2).T - jnp.sum(qmat, 1).T
    grad_c = jnp.dot(dgm, bs, precision=HI)
    grad_b = jnp.dot(dgm.T, cs, precision=HI)
    dwin = jnp.sum(dy * cproj, 2)
    dcum = dcum + dwin * win
    wdy = dy * win[:, :, None]
    grad_c = grad_c + jnp.einsum("ihp,hpn->in", wdy, hin, precision=HI)
    dhin = jnp.einsum("ihp,in->hpn", wdy, cs, precision=HI)
    _, gend = entering((ablk, dhin), "seq", combine, (jnp.ones_like(ablk), empty), True)
    vproj = jnp.einsum("jn,hpn->jhp", bs, gend, precision=HI)
    dwout = jnp.sum(vproj * xdt, 2)
    dxdt = dxdt + vproj * wout[:, :, None]
    grad_b = grad_b + jnp.einsum("jhp,hpn->jn", weighted, gend, precision=HI)
    tail = dwout * wout
    dablk = jnp.sum(gend * hin, (1, 2))
    lastrow = (place == rows - 1)[:, None]
    dcum = dcum - tail + jnp.where(lastrow, (jnp.sum(tail, 0) + dablk * ablk)[None, :], 0.0)
    grad_in = grad_in + dxdt * step_size[:, :, None]
    dstep = jnp.sum(dxdt * xs, 2)
    dla = jnp.flip(jnp.cumsum(jnp.flip(dcum, 0), 0), 0)
    dstep = dstep - rate[None, :] * dla
    part_alog = jnp.sum(dla * la, 0)
    grad_dt = dstep * jax.nn.sigmoid(raw)
    grad_alog, grad_skip, grad_gain = lax.psum((part_alog, part_skip, part_gain), ("seq", "dp"))
    return (
        grad_in.reshape(rows, width).astype(jnp.bfloat16)[None],
        grad_b.astype(jnp.bfloat16)[None],
        grad_c.astype(jnp.bfloat16)[None],
        grad_dt[None],
        grad_alog,
        grad_skip,
        grad_gain,
    )


def solution(mesh):
    return jax.shard_map(
        on_device,
        mesh=mesh,
        in_specs=(
            P(("groups", "dp"), "seq", None),
            P(("groups", "dp"), "seq", None),
            P(("groups", "dp"), "seq", None),
            P(("groups", "dp"), "seq", None),
            P(("groups", "dp"), "seq", None),
            P(),
            P(),
            P(),
            P(("groups", "dp"), None, None),
            P(("groups", "dp"), "seq", None),
        ),
        out_specs=(
            P(("groups", "dp"), "seq", None),
            P(("groups", "dp"), "seq", None),
            P(("groups", "dp"), "seq", None),
            P(("groups", "dp"), "seq", None),
            P("groups"),
            P("groups"),
            P("groups"),
        ),
        check_vma=False,
    )
```

profile of v0, /device:TPU:0, one launch (start us, length us, event | category | flops | bytes accessed | tf_op | source)
XLA Modules:
  0.0 258.3 jit_solution(2906881014786928078)
XLA Ops:
  7.2 0.0 all-gather.6.cloned.1.call-start
  7.3 0.7 slice_bitcast_fusion
  8.0 0.1 compare_reduce_fusion
  8.1 0.1 copy.91
  8.2 0.2 broadcast_in_dim.97
  8.4 0.5 slice.15
  8.9 0.1 reduce.1
  9.0 1.2 fusion.89
  10.2 0.8 compare_select_fusion
  11.0 0.1 copy.92
  11.8 0.2 reduce_window_sum.24
  11.9 0.1 copy.95
  12.0 0.7 broadcast_compare_fusion.1
  12.7 1.3 copy.90
  14.0 0.1 exponential_select_fusion
  14.1 0.1 bitcast_multiply_fusion.3
  14.3 1.6 fusion.68
  15.8 0.0 all-gather.6.cloned.1.call-update
  15.9 0.0 all-gather.8.cloned.1.call-start
  15.9 0.7 copy.93
  16.6 1.2 copy.97
  17.9 1.2 copy.98
  19.1 0.1 mul.290
  19.2 12.6 %all-gather.2 = f32[4,1,64]{2,1,0:T(1,128)S(1)} all-gather(f32[1,1,64]{2,1,0:T(1,128)S(1)} %get-tuple-element.340), channel_id=1, replica_groups=mesh['groups'=2,'seq'=4,'dp'=4] {'seq'}, dimensions={0}, use_global_device_ids=true | all-gather | bytes 1280 | tf_op jit(solution)/shard_map/all_gather | solution.py:12
  31.8 0.1 fusion.62
  31.9 0.1 fusion.71
  32.1 67.4 %all-gather.6.cloned.1.call-done = f32[256,32,128]{2,1,0:T(8,128)} async-done(((f32[64,32,128]{2,1,0:T(8,128)}), f32[256,32,128]{2,1,0:T(8,128)}) %all-gather.6.cloned.1.call-update) | async-done | bytes 4194320 | tf_op jit(solution)/shard_map/all_gather | solution.py:12
  99.5 6.1 %while.30 = (s32[]{:T(128)}, f32[64,32,128]{2,1,0:T(8,128)S(1)}, s32[]{:T(128)}, f32[4,64]{1,0:T(4,128)S(1)}, f32[4,64,32,128]{3,2,1,0:T(8,128)}, /*index=5*/s32[]{:T(128)}, s32[]{:T(128)}) while((s32[]{:T(128)}, f32[64,32,128]{2,1,0:T(8,128)S(1)}, s32[]{:T(128)}, f32[4,64]{1,0:T(4,128)S(1)}, f32[4,64,32,128]{3,2,1,0:T(8,128)}, ...), condition=%wide.region_4.5_spmd.clone, body=%wide.region_3.4_spmd.clone.sunk | while | flops 1048580 | bytes 3146601 | solution.py:25
  99.5 1.5 fusion.104
  101.0 1.5 fusion.104
  102.6 1.5 fusion.104
  104.1 1.5 fusion.104
  105.6 0.6 convolution_bitcast_fusion.1
  106.2 8.4 %multiply_reduce_fusion.6 = (f32[128]{0:T(128)S(1)}, f32[128,64,32]{0,2,1:T(8,128)S(1)}) fusion(f32[128,64,32]{0,2,1:T(8,128)S(1)} %bitcast.171, f32[64]{0:T(128)S(1)} %copy-done.17, f32[128,64,32]{0,2,1:T(8,128)S(1)} %convolution_bitcast_fusion.1, f32[128,64]{0,1:T(8,128)S(1)} %get-tuple-element.343, f32[128,128]{1,0:T(8,128)S(1)} %fusion.71, ...), kind=kOutput, calls=%fused_computation.61 | convolution fusion | flops 409468800 | bytes 3851008 | tf_op jit(solution)/shard_map/hij,jhp->ihp/dot_general | solution.py:63
  114.6 1.4 copy.99
  116.0 2.2 fusion.46
  118.2 2.1 subtract_multiply_fusion
  120.3 1.6 fusion.49
  121.9 0.0 all-gather.8.cloned.1.call-update
  122.0 0.5 iota_compare_fusion.1
  122.5 1.8 convolution_bitcast_fusion.2
  124.3 10.8 %fusion.8 = (f32[64,128]{1,0:T(8,128)}, f32[64,128]{1,0:T(8,128)}, f32[128,128]{1,0:T(8,128)S(1)}) fusion(f32[128,128]{1,0:T(8,128)S(1)} %fusion.71, f32[64,128]{1,0:T(8,128)} %copy.93, pred[128,128]{1,0:T(8,128)(4,1)} %copy-done.13, f32[128,64,32]{0,2,1:T(8,128)S(1)} %subtract_multiply_fusion, f32[128,64]{0,1:T(8,128)S(1)} %get-tuple-element.345, ...), kind=kOutput, calls=%fused_computation.12 | convolution fusion | flops 411533312 | bytes 1851392 | tf_op jit(solution)/shard_map/ihp,jhp->hij/dot_general | solution.py:78
  135.2 0.8 fusion.37
  136.0 65.4 %all-gather.8.cloned.1.call-done = f32[256,32,128]{2,1,0:T(8,128)} async-done(((f32[64,32,128]{2,1,0:T(8,128)}), f32[256,32,128]{2,1,0:T(8,128)}) %all-gather.8.cloned.1.call-update) | async-done | bytes 4194320 | tf_op jit(solution)/shard_map/all_gather | solution.py:12
  201.4 6.1 %while.31 = (s32[]{:T(128)}, f32[64,32,128]{2,1,0:T(8,128)S(1)}, s32[]{:T(128)}, f32[4,64]{1,0:T(4,128)S(1)}, f32[4,64,32,128]{3,2,1,0:T(8,128)}, /*index=5*/s32[]{:T(128)}, s32[]{:T(128)}, s32[]{:T(128)}, s32[]{:T(128)}) while((s32[]{:T(128)}, f32[64,32,128]{2,1,0:T(8,128)S(1)}, s32[]{:T(128)}, f32[4,64]{1,0:T(4,128)S(1)}, ...), condition=%wide.region_8.9_spmd.clone, body=%wide.region_7.8_spmd.clone.sunk | while | flops 1048584 | bytes 3146663 | solution.py:25
  201.4 1.5 fusion.105
  202.9 1.5 fusion.105
  204.5 1.5 fusion.105
  206.0 1.5 fusion.105
  207.6 0.6 convolution_bitcast_fusion
  208.2 0.6 multiply_reduce_fusion.2
  208.8 1.9 convolution_bitcast_fusion.3
  210.7 4.9 %multiply_reduce_fusion.1 = (f32[64]{0:T(128)S(1)}, f32[128,64]{0,1:T(8,128)S(1)}, f32[128,64]{0,1:T(8,128)S(1)}, f32[128,64]{0,1:T(8,128)S(1)}, bf16[128,64,32]{0,2,1:T(8,128)(2,1)S(1)}) fusion(f32[128,64,32]{0,2,1:T(8,128)S(1)} %subtract_multiply_fusion, f32[128,64,32]{0,2,1:T(8,128)S(1)} %convolution_bitcast_fusion, ...), kind=kOutput, calls=%fused_computation.53 | convolution fusion | flops 409968576 | bytes 4473344 | tf_op jit(solution)/shard_map/hij,ihp->jhp/dot_general | solution.py:77
  215.6 0.1 multiply_reduce_fusion.8
  215.7 0.1 fusion.64
  215.8 0.1 rev.7
  215.9 0.1 copy.100
  216.0 0.2 reduce_window_sum.25
  216.2 0.1 copy.101
  216.2 0.1 rev.8
  216.3 0.9 fusion.38
  217.2 1.0 copy.102
  218.2 0.8 multiply_reduce_fusion.7
  219.0 32.4 %all-reduce = (f32[64]{0:T(128)}, f32[64]{0:T(128)}, f32[2048]{0:T(1024)}) all-reduce(f32[64]{0:T(128)S(1)} %get-tuple-element.341, f32[64]{0:T(128)S(1)} %get-tuple-element.311, f32[2048]{0:T(1024)S(1)} %get-tuple-element.309), channel_id=1, replica_groups=mesh['groups'=2,'seq'=4,'dp'=4] {'seq','dp'}, use_global_device_ids=true, to_apply=%region_19.20 | all-reduce | flops 2176 | bytes 17408 | tf_op jit(solution)/shard_map/psum | solution.py:104
  (54 shorter events, 0.2 us)
Async XLA Ops:
  7.2 7.1 %copy-start = (bf16[1,128,128]{2,1,0:T(8,128)(2,1)S(1)}, bf16[1,128,128]{2,1,0:T(8,128)(2,1)}, u32[]{:S(2)}) copy-start(bf16[1,128,128]{2,1,0:T(8,128)(2,1)} %param.16) | copy-start | bytes 98308
  7.2 10.7 %copy-start.4 = (bf16[1,128,2048]{2,1,0:T(8,128)(2,1)S(1)}, bf16[1,128,2048]{2,1,0:T(8,128)(2,1)}, u32[]{:S(2)}) copy-start(bf16[1,128,2048]{2,1,0:T(8,128)(2,1)} %param.23) | copy-start | bytes 1572868
  7.2 92.3 %all-gather.6.cloned.1.call-start = ((), (), s32[]{:S(2)}) async-start(), calls=%async_computation | async-start | bytes 5242880 | tf_op jit(solution)/shard_map/all_gather | solution.py:12
  14.0 85.5 %copy-start.2 = (bf16[1,128,2048]{1,2,0:T(8,128)(2,1)}, bf16[1,128,2048]{1,2,0:T(8,128)(2,1)S(1)}, u32[]{:S(2)}) copy-start(bf16[1,128,2048]{1,2,0:T(8,128)(2,1)S(1)} %copy.90) | copy-start | bytes 1572868
  14.0 5.1 %copy-start.9 = (f32[2048]{0:T(1024)S(1)}, f32[2048]{0:T(1024)}, u32[]{:S(2)}) copy-start(f32[2048]{0:T(1024)} %param.21) | copy-start | bytes 24580
  14.0 17.9 %copy-start.7 = (bf16[1,128,128]{2,1,0:T(8,128)(2,1)S(1)}, bf16[1,128,128]{2,1,0:T(8,128)(2,1)}, u32[]{:S(2)}) copy-start(bf16[1,128,128]{2,1,0:T(8,128)(2,1)} %param.17) | copy-start | bytes 98308
  15.9 185.5 %all-gather.8.cloned.1.call-start = ((), (), s32[]{:S(2)}) async-start(), calls=%async_computation.1 | async-start | bytes 5242880 | tf_op jit(solution)/shard_map/all_gather | solution.py:12
  31.9 74.3 %copy-start.13 = (pred[128,128]{1,0:T(8,128)(4,1)}, pred[128,128]{1,0:T(8,128)(4,1)S(1)}, u32[]{:S(2)}) copy-start(pred[128,128]{1,0:T(8,128)(4,1)S(1)} %fusion.62) | copy-start | bytes 49156
  99.5 6.7 %copy-start.17 = (f32[64]{0:T(128)S(1)}, f32[64]{0:T(128)}, u32[]{:S(2)}) copy-start(f32[64]{0:T(128)} %param.20) | copy-start | bytes 772
  106.2 8.4 %copy-start.5 = (f32[128,64,32]{0,2,1:T(8,128)}, f32[128,64,32]{0,2,1:T(8,128)S(1)}, u32[]{:S(2)}) copy-start(f32[128,64,32]{0,2,1:T(8,128)S(1)} %convolution_bitcast_fusion.1) | copy-start | bytes 3145732
  114.6 3.6 %copy-start.1 = (f32[128,64,32]{0,2,1:T(8,128)}, f32[128,64,32]{0,2,1:T(8,128)S(1)}, u32[]{:S(2)}) copy-start(f32[128,64,32]{0,2,1:T(8,128)S(1)} %get-tuple-element.352) | copy-start | bytes 3145732
  207.5 1.2 copy-start.3
  207.5 3.1 %copy-start.6 = (f32[128,64,32]{0,2,1:T(8,128)S(1)}, f32[128,64,32]{0,2,1:T(8,128)}, u32[]{:S(2)}) copy-start(f32[128,64,32]{0,2,1:T(8,128)} %copy-done.5) | copy-start | bytes 3145732
  207.5 3.1 %copy-start.10 = (f32[64,128]{1,0:T(8,128)S(1)}, f32[64,128]{1,0:T(8,128)}, u32[]{:S(2)}) copy-start(f32[64,128]{1,0:T(8,128)} %copy.93) | copy-start | bytes 98308
  207.6 3.1 %copy-start.14 = (pred[128,128]{1,0:T(8,128)(4,1)S(1)}, pred[128,128]{1,0:T(8,128)(4,1)}, u32[]{:S(2)}) copy-start(pred[128,128]{1,0:T(8,128)(4,1)} %copy-done.13) | copy-start | bytes 49156
  207.6 3.1 %copy-start.18 = (f32[64]{0:T(128)S(1)}, f32[64]{0:T(128)}, u32[]{:S(2)}) copy-start(f32[64]{0:T(128)} %param.20) | copy-start | bytes 772
  210.7 5.0 %copy-start.11 = (f32[64,128]{1,0:T(8,128)S(1)}, f32[64,128]{1,0:T(8,128)}, u32[]{:S(2)}) copy-start(f32[64,128]{1,0:T(8,128)} %get-tuple-element.306) | copy-start | bytes 98308
  210.7 5.0 %copy-start.12 = (f32[64,128]{1,0:T(8,128)S(1)}, f32[64,128]{1,0:T(8,128)}, u32[]{:S(2)}) copy-start(f32[64,128]{1,0:T(8,128)} %get-tuple-element.307) | copy-start | bytes 98308
  210.7 5.0 %copy-start.16 = (pred[128]{0:T(512)(128)(4,1)S(1)}, pred[128]{0:T(512)(128)(4,1)}, u32[]{:S(2)}) copy-start(pred[128]{0:T(512)(128)(4,1)} %iota_compare_fusion.1) | copy-start | bytes 388
  210.7 7.5 %copy-start.8 = (f32[1,128,64]{1,2,0:T(8,128)S(1)}, f32[1,128,64]{1,2,0:T(8,128)}, u32[]{:S(2)}) copy-start(f32[1,128,64]{1,2,0:T(8,128)} %param.18) | copy-start | bytes 98308
  210.7 7.5 %copy-start.15 = (f32[64]{0:T(128)S(1)}, f32[64]{0:T(128)}, u32[]{:S(2)}) copy-start(f32[64]{0:T(128)} %get-tuple-element.347) | copy-start | bytes 772
Sparse Core Ops, SparseCore 0:
  16.0 83.4 all-gather.5
  122.1 79.2 all-gather.7
where the time goes:
time: 259 us; the launch traced here: 258 us
  waiting for transfers between devices  133 us (51%)
  blocking collectives  45.1 us (17%)
  matrix products  34 us (13%)
  other arithmetic  21.9 us (8%)
  between operations  15.1 us (6%)
  local copies, waits for them, and re-layouts  8.92 us (3%)
    all_gather x2, waiting for transfers between devices, entering(): everything = jax.tree.map(lambda part: lax.all_gather(part, axis), shard)  133 us
    psum x1, blocking collectives, on_device(): lax.psum((part_alog, part_skip, part_gain), ('seq', 'dp'))  32.4 us
    all_gather x1, blocking collectives, entering(): everything = jax.tree.map(lambda part: lax.all_gather(part, axis), shard)  12.6 us
    select_n x8, other arithmetic, step(): return jax.tree.map(lambda a, b: jnp.where(reached, a, b), new, before)  11.9 us
    dot_general x1, matrix products, on_device(): dsw = jnp.einsum('ihp,jhp->hij', dy, xdt, precision=HI)  10.8 us
    dot_general x1, matrix products, on_device(): y_intra = jnp.einsum('hij,jhp->ihp', sweights, xdt, precision=HI)  8.38 us
  transfers between devices with their start and end apart: 2, of which 2 were waited for; matrix products, arithmetic and copies ran while one was open for 7% of the time, Pallas kernels for 0%

commit v1 on v0

v1 whole, which is shorter than its diff:
```python
import functools

import jax
import jax.numpy as jnp
from jax import lax
from jax.experimental import pallas as pl
from jax.experimental.pallas import tpu as pltpu
from jax.sharding import PartitionSpec as P

EPS = 1e-05
HI = lax.Precision.HIGHEST
F32 = jnp.float32
BF16 = jnp.bfloat16
MESH = pl.DeviceIdType.MESH
GROUP = 8


def nn(a, b):
    return lax.dot_general(a, b, (((1,), (0,)), ((), ())), preferred_element_type=F32)


def nt(a, b):
    return lax.dot_general(a, b, (((1,), (1,)), ((), ())), preferred_element_type=F32)


def tn(a, b):
    return lax.dot_general(a, b, (((0,), (0,)), ((), ())), preferred_element_type=F32)


def split(a):
    high = a.astype(BF16)
    return high, (a - high.astype(F32)).astype(BF16)


def exact_dot(a, b):
    return jnp.dot(a, b, precision=HI, preferred_element_type=F32)


def kernel(
    peers, dps, heads, hdim, rows,
    x_ref, z_ref, b_ref, c_ref, raw_ref, alog_ref, skip_ref, gain_ref, spans_ref, cot_ref,
    gx_ref, gb_ref, gc_ref, gdt_ref, red_out,
    xt, gate, dnorm, cott, gated, yns, dyt,
    hin, hend, gin, gout,
    ldt, mhigh, mlow, gmat_ref, bias_ref,
    cumr, cumc, dtr, winr, dtwoutr, skipr, ablkr, lar,
    s1, s2, sk, lastr, dgm, gcacc, gbacc, stat,
    part, seq_slots, part2, dp_slots,
    fs_send, fs_recv, bs_send, bs_recv, r1_send, r1_recv, r2_send, r2_recv,
):
    width = heads * hdim
    chunks = heads // GROUP
    span = GROUP * hdim
    tiles = span // 128
    me = lax.axis_index("seq")
    mine = lax.axis_index("dp")
    is_first = me == 0
    is_last = me == peers - 1
    right = jnp.minimum(me + 1, peers - 1)
    left = jnp.maximum(me - 1, 0)

    barrier = pltpu.get_barrier_semaphore()
    for d in range(1, peers):
        pl.semaphore_signal(
            barrier, inc=1, device_id={"seq": lax.rem(me + d, peers)}, device_id_type=MESH
        )
    for d in range(1, dps):
        pl.semaphore_signal(
            barrier, inc=1, device_id={"dp": lax.rem(mine + d, dps)}, device_id_type=MESH
        )

    def forward_copy(k):
        return pltpu.make_async_remote_copy(
            src_ref=hend.at[k], dst_ref=hin.at[k], send_sem=fs_send.at[k],
            recv_sem=fs_recv.at[k], device_id={"seq": right}, device_id_type=MESH,
        )

    def backward_copy(k):
        return pltpu.make_async_remote_copy(
            src_ref=gout.at[k], dst_ref=gin.at[k], send_sem=bs_send.at[k],
            recv_sem=bs_recv.at[k], device_id={"seq": left}, device_id_type=MESH,
        )

    raw = raw_ref[...]
    dt_c = jnp.maximum(raw, 0.0) + jnp.log1p(jnp.exp(-jnp.abs(raw)))
    rate = jnp.exp(alog_ref[...])
    la_c = -rate * dt_c
    both = jnp.concatenate([dt_c, la_c], axis=1).T
    dt = both[:heads]
    la = both[heads:]
    skip_b = jnp.broadcast_to(skip_ref[...], (rows, heads))
    skip_t = jnp.concatenate([skip_b, skip_b], axis=1).T[:heads]
    at_sub = lax.broadcasted_iota(jnp.int32, (rows, rows), 0)
    at_lane = lax.broadcasted_iota(jnp.int32, (rows, rows), 1)
    upper = jnp.where(at_sub <= at_lane, 1.0, 0.0).astype(F32)
    cum = exact_dot(la, upper)
    cum_c = jnp.concatenate([cum, cum], axis=0).T
    offset = me * rows
    seg_sub = jnp.zeros((rows, rows), jnp.int32)
    seg_lane = jnp.zeros((rows, rows), jnp.int32)
    seg_last = jnp.zeros((1, rows), jnp.int32)
    for d in range(spans_ref.shape[0]):
        start = spans_ref[d, 0] - offset
        inside = jnp.where(start >= 0, 1, 0)
        seg_sub = seg_sub + jnp.where(at_sub >= start, inside, 0)
        seg_lane = seg_lane + jnp.where(at_lane >= start, inside, 0)
        seg_last = seg_last + jnp.where(rows - 1 >= start, inside, 0)
    same = (at_sub >= at_lane) & (seg_sub == seg_lane)
    bias_ref[...] = jnp.where(same, 0.0, -jnp.inf)
    seg = seg_lane[:heads]
    cum_end = jnp.broadcast_to(cum[:, rows - 1:rows], (heads, rows))
    win = jnp.where(seg == 0, jnp.exp(cum), 0.0)
    wout = jnp.where(seg == seg_last, jnp.exp(cum_end - cum), 0.0)
    ablk = jnp.where(seg_last == 0, jnp.exp(cum_end), 0.0)
    shape3 = (chunks, GROUP, rows)
    cumr[...] = cum.reshape(shape3)
    dtr[...] = dt.reshape(shape3)
    winr[...] = win.reshape(shape3)
    dtwoutr[...] = (dt * wout).reshape(shape3)
    skipr[...] = skip_t.reshape(shape3)
    ablkr[...] = ablk.reshape(shape3)
    lar[...] = la
    for k in range(chunks):
        cumc[k, :, 0:GROUP] = cum_c[:, k * GROUP:(k + 1) * GROUP]
    bs = b_ref[...]
    cs = c_ref[...]
    gmat_ref[...] = nt(cs, bs)
    b_rows = jnp.concatenate([bs, bs], axis=0)
    b_lanes = jnp.concatenate([bs, bs], axis=1)
    c_rows = jnp.concatenate([cs, cs], axis=0)
    c_lanes = jnp.concatenate([cs, cs], axis=1)

    def per_head(ref, k):
        return jnp.broadcast_to(ref[k][:, None, :], (GROUP, hdim, rows)).reshape(span, rows)

    def over_channels(a):
        return jnp.sum(a.reshape(GROUP, hdim, rows), axis=1)

    def to_tokens_last(ref, k):
        parts = []
        for t in range(tiles):
            at = pl.multiple_of(k * span + t * 128, 128)
            parts.append(ref[:, pl.ds(at, 128)].astype(F32).T)
        return jnp.concatenate(parts, axis=0)

    pl.semaphore_wait(barrier, peers - 1 + dps - 1)

    def local_state(k, carry):
        xk = to_tokens_last(x_ref, k)
        xt[k] = xk.astype(BF16)
        high, low = split(xk * per_head(dtwoutr, k))
        hend[k] = nn(jnp.concatenate([high, low], axis=1), b_rows)

        @pl.when(is_first & (not_alone))
        def _():
            forward_copy(k).start()

        return carry

    not_alone = peers > 1
    lax.fori_loop(0, chunks, local_state, 0)

    @pl.when(is_first)
    def _():
        hin[...] = jnp.zeros(hin.shape, F32)

    @pl.when(is_last)
    def _():
        gin[...] = jnp.zeros(gin.shape, F32)

    stat[...] = jnp.zeros(stat.shape, F32)
    dgm[...] = jnp.zeros(dgm.shape, F32)
    gcacc[...] = jnp.zeros(gcacc.shape, F32)
    gbacc[...] = jnp.zeros(gbacc.shape, F32)

    def forward(k, carry):
        gmat = gmat_ref[...]
        bias = bias_ref[...]
        cc = cumc[k]
        cr = cumr[k]
        dk = dtr[k]
        for q in range(GROUP):
            decay = jnp.exp(cc[:, q:q + 1] - cr[q:q + 1, :] + bias) * dk[q:q + 1, :]
            ldt[k * GROUP + q] = decay
            high, low = split(decay * gmat)
            mhigh[k * GROUP + q] = high
            mlow[k * GROUP + q] = low
            xq = xt[k, q * hdim:(q + 1) * hdim, :]
            yns[k, q * hdim:(q + 1) * hdim, :] = nt(xq, high) + nt(xq, low)
        zk = to_tokens_last(z_ref, k)
        gatek = zk / (1.0 + jnp.exp(-zk))
        gate[k] = gatek
        cotk = to_tokens_last(cot_ref, k)
        cott[k] = cotk
        gparts = []
        for t in range(tiles):
            at = pl.multiple_of(k * span + t * 128, 128)
            gparts.append(jnp.broadcast_to(gain_ref[:, pl.ds(at, 128)], (rows, 128)).T)
        dnormk = cotk * jnp.concatenate(gparts, axis=0)
        dnorm[k] = dnormk

        @pl.when(jnp.logical_not(is_first))
        def _():
            forward_copy(k).wait_recv()
            hend[k] = per_head(ablkr, k) * hin[k] + hend[k]

        @pl.when(jnp.logical_not(is_first) & jnp.logical_not(is_last))
        def _():
            forward_copy(k).start()

        high, low = split(hin[k])
        cproj = nt(jnp.concatenate([high, low], axis=1), c_lanes)
        y = yns[k] + per_head(winr, k) * cproj
        yns[k] = y
        gk = (y + per_head(skipr, k) * xt[k].astype(F32)) * gatek
        gated[k] = gk
        stat[0:1, :] += jnp.sum(gk * gk, axis=0, keepdims=True)
        stat[1:2, :] += jnp.sum(gk * dnormk, axis=0, keepdims=True)
        return carry

    lax.fori_loop(0, chunks, forward, 0)

    scale = lax.rsqrt(stat[0:1, :] / width + EPS)
    mean = scale * stat[1:2, :] / width
    ones8 = jnp.ones((8, rows), BF16)

    def middle(k, carry):
        normed = gated[k] * scale
        dy = scale * (dnorm[k] - normed * mean) * gate[k]
        dyt[k] = dy
        high, low = split(dy * per_head(winr, k))
        gout[k] = nn(jnp.concatenate([high, low], axis=1), c_rows)

        @pl.when(is_last & (not_alone))
        def _():
            backward_copy(k).start()

        return carry

    lax.fori_loop(0, chunks, middle, 0)

    def backward(k, carry):
        dyk = dyt[k]
        dhigh, dlow = split(dyk)
        xk = xt[k]
        dx_parts = []
        total = dgm[...]
        for q in range(GROUP):
            sl = slice(q * hdim, (q + 1) * hdim)
            dh, dl, xq = dhigh[sl], dlow[sl], xk[sl]
            prod = tn(jnp.concatenate([dh, dl], axis=0), jnp.concatenate([xq, xq], axis=0))
            total = total + prod * ldt[k * GROUP + q]
            mh = mhigh[k * GROUP + q]
            ml = mlow[k * GROUP + q]
            dx_parts.append(nn(jnp.concatenate([dh, dl], axis=1), jnp.concatenate([mh, mh], axis=0)) + nn(dh, ml))
        dgm[...] = total
        dx = jnp.concatenate(dx_parts, axis=0)
        xf = xk.astype(F32)
        normed = gated[k] * scale
        ph, plo = split(cott[k] * normed)
        row = nt(ones8, ph) + nt(ones8, plo)
        for t in range(tiles):
            part[pl.ds(k * tiles + t, 1), :] = row[0:1, t * 128:(t + 1) * 128]
        s1[k] = over_channels(dyk * yns[k])
        sk[k] = over_channels(dyk * xf)
        wh, wl = split(dyk * per_head(winr, k))
        hh, hl = split(hin[k])
        gcacc[...] += tn(wh, hh) + tn(wh, hl) + tn(wl, hh)

        @pl.when(jnp.logical_not(is_last))
        def _():
            backward_copy(k).wait_recv()
            gout[k] = per_head(ablkr, k) * gin[k] + gout[k]

        @pl.when(jnp.logical_not(is_first) & jnp.logical_not(is_last))
        def _():
            backward_copy(k).start()

        gend = gin[k]
        gh, gl = split(gend)
        vproj = nt(jnp.concatenate([gh, gl], axis=1), b_lanes)
        weight = per_head(dtwoutr, k)
        dx = dx + weight * vproj
        uh, ul = split(xf * weight)
        gbacc[...] += tn(uh, gh) + tn(uh, gl) + tn(ul, gh)
        s2[k] = over_channels(dx * xf)
        lastr[k] = over_channels(gend * hend[k])
        gx = dx + per_head(skipr, k) * dyk
        for t in range(tiles):
            at = pl.multiple_of(k * span + t * 128, 128)
            gx_ref[:, pl.ds(at, 128)] = gx[t * 128:(t + 1) * 128].T.astype(BF16)
        return carry

    lax.fori_loop(0, chunks, backward, 0)

    rows_of = s2[...].reshape(heads, rows)
    dcum = s1[...].reshape(heads, rows) - rows_of
    lower = jnp.where(at_sub >= at_lane, 1.0, 0.0).astype(F32)
    dla = exact_dot(dcum, lower) + exact_dot(
        lastr[...].reshape(heads, rows), jnp.ones((rows, rows), F32)
    )
    dtall = dtr[...].reshape(heads, rows)
    sums = jnp.concatenate([sk[...].reshape(heads, rows), dla * lar[...]], axis=0)
    tail = lax.dot_general(
        jnp.ones((8, rows), F32), sums, (((1,), (1,)), ((), ())),
        precision=HI, preferred_element_type=F32,
    )
    gain_rows = width // 128
    part[gain_rows:gain_rows + 8, :] = tail

    def exchange(axis, n, position, src, slots, send, recv):
        def copy(d):
            return pltpu.make_async_remote_copy(
                src_ref=src, dst_ref=slots.at[position], send_sem=send.at[d],
                recv_sem=recv.at[d], device_id={axis: lax.rem(position + d, n)},
                device_id_type=MESH,
            )

        for d in range(1, n):
            copy(d).start()
        slots[position] = src[...]
        return copy

    def collect(n, position, slots, send, recv, src):
        for d in range(1, n):
            pltpu.make_async_remote_copy(
                src_ref=src, dst_ref=slots.at[lax.rem(position - d + n, n)],
                send_sem=send.at[d], recv_sem=recv.at[d],
                device_id={"seq": right}, device_id_type=MESH,
            ).wait_recv()
        total = slots[0]
        for d in range(1, n):
            total = total + slots[d]
        return total

    copy1 = exchange("seq", peers, me, part, seq_slots, r1_send, r1_recv)

    back = jnp.concatenate([rows_of / dtall, dla], axis=0).T
    sig = 1.0 / (1.0 + jnp.exp(-raw))
    gdt_ref[...] = (back[:, :heads] - rate * back[:, heads:]) * sig
    dg_high, dg_low = split(dgm[...])
    gc_ref[...] = (gcacc[...] + nn(dg_high, bs) + nn(dg_low, bs)).astype(BF16)
    gb_ref[...] = (gbacc[...] + tn(dg_high, cs) + tn(dg_low, cs)).astype(BF16)

    part2[...] = collect(peers, me, seq_slots, r1_send, r1_recv, part)
    copy2 = exchange("dp", dps, mine, part2, dp_slots, r2_send, r2_recv)
    red_out[...] = collect(dps, mine, dp_slots, r2_send, r2_recv, part2)
    for d in range(1, peers):
        copy1(d).wait_send()
    for d in range(1, dps):
        copy2(d).wait_send()

    @pl.when(jnp.logical_not(is_last))
    def _():
        @pl.loop(0, chunks)
        def _(k):
            forward_copy(k).wait_send()

    @pl.when(jnp.logical_not(is_first))
    def _():
        @pl.loop(0, chunks)
        def _(k):
            backward_copy(k).wait_send()


def on_device(peers, dps, scan_input, gate_input, bmat, cmat, dt_raw, a_log, d_skip, gain, spans, cot):
    rows, width = scan_input.shape[1:]
    heads = a_log.shape[0]
    hdim = width // heads
    state = bmat.shape[2]
    chunks = heads // GROUP
    span = GROUP * hdim
    red_rows = width // 128 + 8
    vmem = pl.BlockSpec(memory_space=pltpu.VMEM)
    wide = lambda dtype=F32: pltpu.VMEM((chunks, span, rows), dtype)
    states = pltpu.VMEM((chunks, span, state), F32)
    small = pltpu.VMEM((chunks, GROUP, rows), F32)
    square = pltpu.VMEM((rows, rows), F32)
    dma = pltpu.SemaphoreType.DMA
    gx, gb, gc, gdt, red = pl.pallas_call(
        functools.partial(kernel, peers, dps, heads, hdim, rows),
        out_shape=(
            jax.ShapeDtypeStruct((rows, width), BF16),
            jax.ShapeDtypeStruct((rows, state), BF16),
            jax.ShapeDtypeStruct((rows, state), BF16),
            jax.ShapeDtypeStruct((rows, heads), F32),
            jax.ShapeDtypeStruct((red_rows, 128), F32),
        ),
        in_specs=[vmem] * 8 + [pl.BlockSpec(memory_space=pltpu.SMEM), vmem],
        out_specs=(vmem,) * 5,
        scratch_shapes=[
            wide(BF16), wide(), wide(), wide(), wide(), wide(), wide(),
            states, states, states, states,
            pltpu.VMEM((heads, rows, rows), F32),
            pltpu.VMEM((heads, rows, rows), BF16),
            pltpu.VMEM((heads, rows, rows), BF16),
            square, square,
            small, pltpu.VMEM((chunks, rows, 128), F32), small, small, small, small, small,
            pltpu.VMEM((heads, rows), F32),
            small, small, small, small,
            square, pltpu.VMEM((rows, state), F32), pltpu.VMEM((rows, state), F32),
            pltpu.VMEM((8, rows), F32),
            pltpu.VMEM((red_rows, 128), F32),
            pltpu.VMEM((peers, red_rows, 128), F32),
            pltpu.VMEM((red_rows, 128), F32),
            pltpu.VMEM((dps, red_rows, 128), F32),
            dma((chunks,)), dma((chunks,)), dma((chunks,)), dma((chunks,)),
            dma((peers,)), dma((peers,)), dma((dps,)), dma((dps,)),
        ],
        compiler_params=pltpu.CompilerParams(
            collective_id=0, has_side_effects=True, vmem_limit_bytes=56 * 1024 * 1024
        ),
        name="scan_layer",
    )(
        scan_input[0], gate_input[0], bmat[0], cmat[0], dt_raw[0],
        a_log[None], d_skip[None], gain[None], spans[0], cot[0],
    )
    gain_rows = width // 128
    return (
        gx[None], gb[None], gc[None], gdt[None],
        red[gain_rows, heads:2 * heads],
        red[gain_rows, :heads],
        red[:gain_rows].reshape(width),
    )


def solution(mesh):
    return jax.shard_map(
        functools.partial(on_device, mesh.shape["seq"], mesh.shape["dp"]),
        mesh=mesh,
        in_specs=(
            P(("groups", "dp"), "seq", None),
            P(("groups", "dp"), "seq", None),
            P(("groups", "dp"), "seq", None),
            P(("groups", "dp"), "seq", None),
            P(("groups", "dp"), "seq", None),
            P(),
            P(),
            P(),
            P(("groups", "dp"), None, None),
            P(("groups", "dp"), "seq", None),
        ),
        out_specs=(
            P(("groups", "dp"), "seq", None),
            P(("groups", "dp"), "seq", None),
            P(("groups", "dp"), "seq", None),
            P(("groups", "dp"), "seq", None),
            P("groups"),
            P("groups"),
            P("groups"),
        ),
        check_vma=False,
    )
```

time: 259 us -> 91.5 us (0.35)
  waiting for transfers between devices: 133 us -> 0 us
  Pallas kernels: 0 us -> 79.2 us
  blocking collectives: 45.1 us -> 0 us
  matrix products: 34 us -> 0 us
  other arithmetic: 21.9 us -> 0 us
  between operations: 15.1 us -> 0.65 us
    all_gather x2 -> x0, waiting for transfers between devices: 133 us -> none  [entering(): everything = jax.tree.map(lambda part: lax.all_gather(part, axis), shard)]
    pallas_call x0 -> x1, Pallas kernels: none -> 79.2 us  [on_device(): pl.pallas_call(functools.partial(kernel, peers, dps, heads, hdim, rows),...]
    dot_general x12 -> x0, matrix products: 34 us -> none  [the longest x1 10.8 us: on_device(): dsw = jnp.einsum('ihp,jhp->hij', dy, xdt, precision=HI)]
    psum x1 -> x0, blocking collectives: 32.4 us -> none  [on_device(): lax.psum((part_alog, part_skip, part_gain), ('seq', 'dp'))]
    select_n x10 -> x0, other arithmetic: 12.8 us -> none  [the longest x8 11.9 us: step(): return jax.tree.map(lambda a, b: jnp.where(reached, a, b), new, before)]
    all_gather x1 -> x0, blocking collectives: 12.6 us -> none  [entering(): everything = jax.tree.map(lambda part: lax.all_gather(part, axis), shard)]
    unnamed x40 -> x11, local copies, waits for them, and re-layouts: 2.42 us -> 6.98 us
    reduce_sum x4 -> x0, other arithmetic: 3.63 us -> none  [the longest x1 2.17 us: on_device(): part_gain = jnp.sum(upstream * normed, 0)]
  transfers between devices with their start and end apart: 2 -> 0, of which waited for: 2 -> 0; matrix products, arithmetic and copies ran while one was open for 7% -> 0% of each run, Pallas kernels for 0% -> 0%
where the time goes in v1:
time: 91.5 us; the launch traced here: 90.2 us
  Pallas kernels  79.2 us (87%)
  local copies, waits for them, and re-layouts  10.3 us (11%)
    pallas_call x1, Pallas kernels, on_device(): pl.pallas_call(functools.partial(kernel, peers, dps, heads, hdim, rows),...  79.2 us
    unnamed x11, local copies, waits for them, and re-layouts  6.98 us

profile of v1, /device:TPU:0, one launch (start us, length us, event | category | flops | bytes accessed | tf_op | source)
XLA Modules:
  0.0 90.2 jit_solution(4910534856334925252)
XLA Ops:
  0.6 1.5 %copy.17 = f32[1,128,64]{2,1,0:T(8,128)} copy(f32[1,128,64]{1,2,0:T(8,128)} %param.14) | data formatting | bytes 65536 | tf_op args[4]
  2.1 0.0 copy-start.2
  2.1 0.7 copy-done.2
  2.8 0.7 copy.18.spans_ref
  3.5 79.2 %scan_layer.1 = (bf16[128,2048]{1,0:T(8,128)(2,1)}, bf16[128,128]{1,0:T(8,128)(2,1)}, bf16[128,128]{1,0:T(8,128)(2,1)}, f32[128,64]{1,0:T(8,128)}, f32[24,128]{1,0:T(8,128)}) custom-call(bf16[128,2048]{1,0:T(8,128)(2,1)} %bitcast.20, bf16[128,2048]{1,0:T(8,128)(2,1)} %bitcast.21, bf16[128,128]{1,0:T(8,128)(2,1)} %bitcast.26, bf16[128,128]{1,0:T(8,128)(2,1)} %bitcast.27, ...), custom_call_target="tpu_custom_call" | custom-call | tf_op jit(solution)/shard_map/scan_layer/pallas_call | solution.py:380
  82.7 1.3 %slice_bitcast_fusion.1 = (f32[64]{0:T(128)}, f32[64]{0:T(128)}) fusion(f32[24,128]{1,0:T(8,128)} %get-tuple-element.16), kind=kLoop, calls=%fused_computation.1 | loop fusion | bytes 1024 | tf_op jit(solution)/shard_map/squeeze | solution.py:422
  84.0 1.3 %slice_bitcast_fusion = f32[2048]{0:T(1024)} fusion(f32[24,128]{1,0:T(8,128)} %get-tuple-element.16), kind=kLoop, calls=%fused_computation | loop fusion | bytes 16384 | tf_op jit(solution)/shard_map/reshape | solution.py:423
  85.3 1.5 %copy.19 = f32[1,128,64]{1,2,0:T(8,128)} copy(f32[1,128,64]{2,1,0:T(8,128)} %bitcast.25) | data formatting | bytes 65536
  86.9 0.0 copy-start.1
  86.9 1.9 %copy.23 = bf16[1,128,2048]{2,1,0:T(8,128)(2,1)} copy(bf16[1,128,2048]{2,1,0:T(8,128)(2,1)} %bitcast.23) | data formatting | bytes 1048576
  88.8 0.0 copy-done.1
  88.8 0.0 copy-start
  88.8 0.6 copy.24
  89.4 0.2 copy-done
  89.5 0.6 copy.25
Async XLA Ops:
  2.1 0.7 copy-start.2
  86.9 1.9 %copy-start.1 = (bf16[128,128]{1,0:T(8,128)(2,1)S(1)}, bf16[128,128]{1,0:T(8,128)(2,1)}, u32[]{:S(2)}) copy-start(bf16[128,128]{1,0:T(8,128)(2,1)} %get-tuple-element.13) | copy-start | bytes 98308
  88.8 0.8 copy-start

commit v2 on v1

--- a/solution.py
+++ b/solution.py
@@ -13,6 +13,7 @@
 BF16 = jnp.bfloat16
 MESH = pl.DeviceIdType.MESH
 GROUP = 8
+PIECES = 4
 
 
 def nn(a, b):
@@ -39,14 +40,14 @@
 def kernel(
     peers, dps, heads, hdim, rows,
     x_ref, z_ref, b_ref, c_ref, raw_ref, alog_ref, skip_ref, gain_ref, spans_ref, cot_ref,
-    gx_ref, gb_ref, gc_ref, gdt_ref, red_out,
+    gx_ref, gb_ref, gc_ref, gdt_ref, gain_out, skip_out, alog_out,
     xt, gate, dnorm, cott, gated, yns, dyt,
     hin, hend, gin, gout,
     ldt, mhigh, mlow, gmat_ref, bias_ref,
     cumr, cumc, dtr, winr, dtwoutr, skipr, ablkr, lar,
     s1, s2, sk, lastr, dgm, gcacc, gbacc, stat,
-    part, seq_slots, part2, dp_slots,
-    fs_send, fs_recv, bs_send, bs_recv, r1_send, r1_recv, r2_send, r2_recv,
+    part, seq_slots, part2, dp_slots, part3, all_slots,
+    fs_send, fs_recv, bs_send, bs_recv, r1_send, r1_recv, r2_send, r2_recv, r3_send, r3_recv,
 ):
     width = heads * hdim
     chunks = heads // GROUP
@@ -59,37 +60,52 @@
     right = jnp.minimum(me + 1, peers - 1)
     left = jnp.maximum(me - 1, 0)
 
+    team = peers * dps
+
+    def teammate(d):
+        return {"seq": lax.rem(me + d // dps, peers), "dp": lax.rem(mine + d % dps, dps)}
+
     barrier = pltpu.get_barrier_semaphore()
-    for d in range(1, peers):
-        pl.semaphore_signal(
-            barrier, inc=1, device_id={"seq": lax.rem(me + d, peers)}, device_id_type=MESH
+
+    @pl.loop(1, team)
+    def _(d):
+        pl.semaphore_signal(barrier, inc=1, device_id=teammate(d), device_id_type=MESH)
+
+    piece = span // PIECES
+
+    def forward_copy(k, s):
+        at = pl.ds(s * piece, piece)
+        return pltpu.make_async_remote_copy(
+            src_ref=hend.at[k, at], dst_ref=hin.at[k, at], send_sem=fs_send.at[k, s],
+            recv_sem=fs_recv.at[k, s], device_id={"seq": right}, device_id_type=MESH,
         )
-    for d in range(1, dps):
-        pl.semaphore_signal(
-            barrier, inc=1, device_id={"dp": lax.rem(mine + d, dps)}, device_id_type=MESH
+
+    def backward_copy(k, s):
+        at = pl.ds(s * piece, piece)
+        return pltpu.make_async_remote_copy(
+            src_ref=gout.at[k, at], dst_ref=gin.at[k, at], send_sem=bs_send.at[k, s],
+            recv_sem=bs_recv.at[k, s], device_id={"seq": left}, device_id_type=MESH,
         )
 
-    def forward_copy(k):
-        return pltpu.make_async_remote_copy(
-            src_ref=hend.at[k], dst_ref=hin.at[k], send_sem=fs_send.at[k],
-            recv_sem=fs_recv.at[k], device_id={"seq": right}, device_id_type=MESH,
-        )
-
-    def backward_copy(k):
-        return pltpu.make_async_remote_copy(
-            src_ref=gout.at[k], dst_ref=gin.at[k], send_sem=bs_send.at[k],
-            recv_sem=bs_recv.at[k], device_id={"seq": left}, device_id_type=MESH,
-        )
+    def relay(copy, k, source, target, ends):
+        keep = per_head(ablkr, k)
+        for s in range(PIECES):
+            at = slice(s * piece, (s + 1) * piece)
+            copy(k, s).wait_recv()
+            target[k, at, :] = keep[at] * source[k, at, :] + target[k, at, :]
+
+            @pl.when(jnp.logical_not(ends))
+            def _():
+                copy(k, s).start()
 
     raw = raw_ref[...]
-    dt_c = jnp.maximum(raw, 0.0) + jnp.log1p(jnp.exp(-jnp.abs(raw)))
-    rate = jnp.exp(alog_ref[...])
-    la_c = -rate * dt_c
-    both = jnp.concatenate([dt_c, la_c], axis=1).T
-    dt = both[:heads]
-    la = both[heads:]
+    dt = jnp.maximum(raw, 0.0) + jnp.log1p(jnp.exp(-jnp.abs(raw)))
+    rate_b = jnp.broadcast_to(jnp.exp(alog_ref[...]), (rows, heads))
     skip_b = jnp.broadcast_to(skip_ref[...], (rows, heads))
-    skip_t = jnp.concatenate([skip_b, skip_b], axis=1).T[:heads]
+    by_head = jnp.concatenate([skip_b, rate_b], axis=1).T
+    skip_t = by_head[:heads]
+    rate = by_head[heads:]
+    la = -rate * dt
     at_sub = lax.broadcasted_iota(jnp.int32, (rows, rows), 0)
     at_lane = lax.broadcasted_iota(jnp.int32, (rows, rows), 1)
     upper = jnp.where(at_sub <= at_lane, 1.0, 0.0).astype(F32)
@@ -99,8 +115,8 @@
     seg_sub = jnp.zeros((rows, rows), jnp.int32)
     seg_lane = jnp.zeros((rows, rows), jnp.int32)
     seg_last = jnp.zeros((1, rows), jnp.int32)
-    for d in range(spans_ref.shape[0]):
-        start = spans_ref[d, 0] - offset
+    for d in range(spans_ref.shape[1]):
+        start = spans_ref[0, d] - offset
         inside = jnp.where(start >= 0, 1, 0)
         seg_sub = seg_sub + jnp.where(at_sub >= start, inside, 0)
         seg_lane = seg_lane + jnp.where(at_lane >= start, inside, 0)
@@ -143,7 +159,7 @@
             parts.append(ref[:, pl.ds(at, 128)].astype(F32).T)
         return jnp.concatenate(parts, axis=0)
 
-    pl.semaphore_wait(barrier, peers - 1 + dps - 1)
+    pl.semaphore_wait(barrier, team - 1)
 
     def local_state(k, carry):
         xk = to_tokens_last(x_ref, k)
@@ -153,7 +169,8 @@
 
         @pl.when(is_first & (not_alone))
         def _():
-            forward_copy(k).start()
+            for s in range(PIECES):
+                forward_copy(k, s).start()
 
         return carry
 
@@ -201,12 +218,7 @@
 
         @pl.when(jnp.logical_not(is_first))
         def _():
-            forward_copy(k).wait_recv()
-            hend[k] = per_head(ablkr, k) * hin[k] + hend[k]
-
-        @pl.when(jnp.logical_not(is_first) & jnp.logical_not(is_last))
-        def _():
-            forward_copy(k).start()
+            relay(forward_copy, k, hin, hend, is_last)
 
         high, low = split(hin[k])
         cproj = nt(jnp.concatenate([high, low], axis=1), c_lanes)
@@ -233,11 +245,54 @@
 
         @pl.when(is_last & (not_alone))
         def _():
-            backward_copy(k).start()
-
+            for s in range(PIECES):
+                backward_copy(k, s).start()
+
+        ph, plo = split(cott[k] * normed)
+        row = nt(ones8, ph) + nt(ones8, plo)
+        for t in range(tiles):
+            part[pl.ds(k * tiles + t, 1), :] = row[0:1, t * 128:(t + 1) * 128]
+        sk[k] = over_channels(dy * xt[k].astype(F32))
         return carry
 
     lax.fori_loop(0, chunks, middle, 0)
+
+    def lane_sums(a):
+        return lax.dot_general(
+            jnp.ones((8, rows), F32), a, (((1,), (1,)), ((), ())),
+            precision=HI, preferred_element_type=F32,
+        )
+
+    gain_rows = width // 128
+    part[gain_rows:gain_rows + 8, 0:heads] = lane_sums(sk[...].reshape(heads, rows))
+    part[gain_rows:gain_rows + 8, heads:128] = jnp.zeros((8, 128 - heads), F32)
+
+    def exchange(axis, n, position, src, slots, send, recv):
+        def copy(d):
+            return pltpu.make_async_remote_copy(
+                src_ref=src, dst_ref=slots.at[position], send_sem=send.at[d],
+                recv_sem=recv.at[d], device_id={axis: lax.rem(position + d, n)},
+                device_id_type=MESH,
+            )
+
+        for d in range(1, n):
+            copy(d).start()
+        slots[position] = src[...]
+        return copy
+
+    def collect(n, position, slots, send, recv, src):
+        for d in range(1, n):
+            pltpu.make_async_remote_copy(
+                src_ref=src, dst_ref=slots.at[lax.rem(position - d + n, n)],
+                send_sem=send.at[d], recv_sem=recv.at[d],
+                device_id={"seq": right}, device_id_type=MESH,
+            ).wait_recv()
+        total = slots[0]
+        for d in range(1, n):
+            total = total + slots[d]
+        return total
+
+    copy1 = exchange("seq", peers, me, part, seq_slots, r1_send, r1_recv)
 
     def backward(k, carry):
         dyk = dyt[k]
@@ -256,25 +311,14 @@
         dgm[...] = total
         dx = jnp.concatenate(dx_parts, axis=0)
         xf = xk.astype(F32)
-        normed = gated[k] * scale
-        ph, plo = split(cott[k] * normed)
-        row = nt(ones8, ph) + nt(ones8, plo)
-        for t in range(tiles):
-            part[pl.ds(k * tiles + t, 1), :] = row[0:1, t * 128:(t + 1) * 128]
         s1[k] = over_channels(dyk * yns[k])
-        sk[k] = over_channels(dyk * xf)
         wh, wl = split(dyk * per_head(winr, k))
         hh, hl = split(hin[k])
         gcacc[...] += tn(wh, hh) + tn(wh, hl) + tn(wl, hh)
 
         @pl.when(jnp.logical_not(is_last))
         def _():
-            backward_copy(k).wait_recv()
-            gout[k] = per_head(ablkr, k) * gin[k] + gout[k]
-
-        @pl.when(jnp.logical_not(is_first) & jnp.logical_not(is_last))
-        def _():
-            backward_copy(k).start()
+            relay(backward_copy, k, gin, gout, is_first)
 
         gend = gin[k]
         gh, gl = split(gend)
@@ -293,58 +337,47 @@
 
     lax.fori_loop(0, chunks, backward, 0)
 
+    part2[...] = collect(peers, me, seq_slots, r1_send, r1_recv, part)
+    copy2 = exchange("dp", dps, mine, part2, dp_slots, r2_send, r2_recv)
+
     rows_of = s2[...].reshape(heads, rows)
     dcum = s1[...].reshape(heads, rows) - rows_of
     lower = jnp.where(at_sub >= at_lane, 1.0, 0.0).astype(F32)
     dla = exact_dot(dcum, lower) + exact_dot(
         lastr[...].reshape(heads, rows), jnp.ones((rows, rows), F32)
     )
-    dtall = dtr[...].reshape(heads, rows)
-    sums = jnp.concatenate([sk[...].reshape(heads, rows), dla * lar[...]], axis=0)
-    tail = lax.dot_general(
-        jnp.ones((8, rows), F32), sums, (((1,), (1,)), ((), ())),
-        precision=HI, preferred_element_type=F32,
-    )
-    gain_rows = width // 128
-    part[gain_rows:gain_rows + 8, :] = tail
-
-    def exchange(axis, n, position, src, slots, send, recv):
-        def copy(d):
-            return pltpu.make_async_remote_copy(
-                src_ref=src, dst_ref=slots.at[position], send_sem=send.at[d],
-                recv_sem=recv.at[d], device_id={axis: lax.rem(position + d, n)},
-                device_id_type=MESH,
-            )
-
-        for d in range(1, n):
-            copy(d).start()
-        slots[position] = src[...]
-        return copy
-
-    def collect(n, position, slots, send, recv, src):
-        for d in range(1, n):
-            pltpu.make_async_remote_copy(
-                src_ref=src, dst_ref=slots.at[lax.rem(position - d + n, n)],
-                send_sem=send.at[d], recv_sem=recv.at[d],
-                device_id={"seq": right}, device_id_type=MESH,
-            ).wait_recv()
-        total = slots[0]
-        for d in range(1, n):
-            total = total + slots[d]
-        return total
-
-    copy1 = exchange("seq", peers, me, part, seq_slots, r1_send, r1_recv)
-
-    back = jnp.concatenate([rows_of / dtall, dla], axis=0).T
-    sig = 1.0 / (1.0 + jnp.exp(-raw))
-    gdt_ref[...] = (back[:, :heads] - rate * back[:, heads:]) * sig
+    part3[:, 0:heads] = lane_sums(dla * lar[...])[0:1]
+    part3[:, heads:128] = jnp.zeros((1, 128 - heads), F32)
+    number = me * dps + mine
+
+    def team_copy(d):
+        return pltpu.make_async_remote_copy(
+            src_ref=part3, dst_ref=all_slots.at[number], send_sem=r3_send,
+            recv_sem=r3_recv, device_id=teammate(d), device_id_type=MESH,
+        )
+
+    @pl.loop(1, team)
+    def _(d):
+        team_copy(d).start()
+
+    all_slots[number] = part3[...]
+    gdt_ref[...] = (rows_of / dtr[...].reshape(heads, rows) - rate * dla) / (1.0 + jnp.exp(-raw))
     dg_high, dg_low = split(dgm[...])
     gc_ref[...] = (gcacc[...] + nn(dg_high, bs) + nn(dg_low, bs)).astype(BF16)
     gb_ref[...] = (gbacc[...] + tn(dg_high, cs) + tn(dg_low, cs)).astype(BF16)
 
-    part2[...] = collect(peers, me, seq_slots, r1_send, r1_recv, part)
-    copy2 = exchange("dp", dps, mine, part2, dp_slots, r2_send, r2_recv)
-    red_out[...] = collect(dps, mine, dp_slots, r2_send, r2_recv, part2)
+    total = collect(dps, mine, dp_slots, r2_send, r2_recv, part2)
+    gain_out[...] = total[0:gain_rows]
+    skip_out[...] = total[gain_rows:gain_rows + 1, 0:heads]
+    if team > 1:
+        everyone = pltpu.make_async_copy(
+            all_slots.at[pl.ds(0, team - 1)], all_slots.at[pl.ds(1, team - 1)], r3_recv
+        )
+        everyone.wait()
+        pltpu.make_async_copy(
+            all_slots.at[pl.ds(0, team - 1)], all_slots.at[pl.ds(1, team - 1)], r3_send
+        ).wait()
+    alog_out[...] = jnp.sum(all_slots[...], axis=0)[:, 0:heads]
     for d in range(1, peers):
         copy1(d).wait_send()
     for d in range(1, dps):
@@ -354,13 +387,21 @@
     def _():
         @pl.loop(0, chunks)
         def _(k):
-            forward_copy(k).wait_send()
+            for s in range(PIECES):
+                forward_copy(k, s).wait_send()
 
     @pl.when(jnp.logical_not(is_first))
     def _():
         @pl.loop(0, chunks)
         def _(k):
-            backward_copy(k).wait_send()
+            for s in range(PIECES):
+                backward_copy(k, s).wait_send()
+
+
+def hand_over(*refs):
+    n = len(refs) // 2
+    for source, target in zip(refs[:n], refs[n:]):
+        target[...] = source[...]
 
 
 def on_device(peers, dps, scan_input, gate_input, bmat, cmat, dt_raw, a_log, d_skip, gain, spans, cot):
@@ -377,17 +418,19 @@
     small = pltpu.VMEM((chunks, GROUP, rows), F32)
     square = pltpu.VMEM((rows, rows), F32)
     dma = pltpu.SemaphoreType.DMA
-    gx, gb, gc, gdt, red = pl.pallas_call(
+    grads = pl.pallas_call(
         functools.partial(kernel, peers, dps, heads, hdim, rows),
         out_shape=(
             jax.ShapeDtypeStruct((rows, width), BF16),
             jax.ShapeDtypeStruct((rows, state), BF16),
             jax.ShapeDtypeStruct((rows, state), BF16),
-            jax.ShapeDtypeStruct((rows, heads), F32),
-            jax.ShapeDtypeStruct((red_rows, 128), F32),
+            jax.ShapeDtypeStruct((heads, rows), F32),
+            jax.ShapeDtypeStruct((width // 128, 128), F32),
+            jax.ShapeDtypeStruct((1, heads), F32),
+            jax.ShapeDtypeStruct((1, heads), F32),
         ),
         in_specs=[vmem] * 8 + [pl.BlockSpec(memory_space=pltpu.SMEM), vmem],
-        out_specs=(vmem,) * 5,
+        out_specs=(vmem,) * 7,
         scratch_shapes=[
             wide(BF16), wide(), wide(), wide(), wide(), wide(), wide(),
             states, states, states, states,
@@ -404,23 +447,29 @@
             pltpu.VMEM((peers, red_rows, 128), F32),
             pltpu.VMEM((red_rows, 128), F32),
             pltpu.VMEM((dps, red_rows, 128), F32),
-            dma((chunks,)), dma((chunks,)), dma((chunks,)), dma((chunks,)),
-            dma((peers,)), dma((peers,)), dma((dps,)), dma((dps,)),
+            pltpu.VMEM((1, 128), F32),
+            pltpu.VMEM((peers * dps, 1, 128), F32),
+            dma((chunks, PIECES)), dma((chunks, PIECES)), dma((chunks, PIECES)), dma((chunks, PIECES)),
+            dma((peers,)), dma((peers,)), dma((dps,)), dma((dps,)), dma, dma,
         ],
         compiler_params=pltpu.CompilerParams(
             collective_id=0, has_side_effects=True, vmem_limit_bytes=56 * 1024 * 1024
         ),
         name="scan_layer",
     )(
-        scan_input[0], gate_input[0], bmat[0], cmat[0], dt_raw[0],
-        a_log[None], d_skip[None], gain[None], spans[0], cot[0],
+        scan_input[0], gate_input[0], bmat[0], cmat[0], dt_raw[0].T,
+        a_log[None], d_skip[None], gain[None], spans[0].T, cot[0],
     )
-    gain_rows = width // 128
+    gx, gb, gc, gdt, ggain, gskip, galog = pl.pallas_call(
+        hand_over,
+        out_shape=tuple(jax.ShapeDtypeStruct(g.shape, g.dtype) for g in grads),
+        in_specs=[vmem] * len(grads),
+        out_specs=(vmem,) * len(grads),
+        name="hand_over",
+    )(*grads)
     return (
-        gx[None], gb[None], gc[None], gdt[None],
-        red[gain_rows, heads:2 * heads],
-        red[gain_rows, :heads],
-        red[:gain_rows].reshape(width),
+        gx[None], gb[None], gc[None], gdt.T[None],
+        galog.reshape(heads), gskip.reshape(heads), ggain.reshape(width),
     )
 
 

time: 91.5 us -> 77.5 us (0.85); the launches traced: 90.2 us -> 77.3 us
  local copies, waits for them, and re-layouts: 10.3 us -> 0 us
  Pallas kernels: 79.2 us -> 76.7 us
    unnamed x11 -> x0, local copies, waits for them, and re-layouts: 6.98 us -> none
    pallas_call x1, Pallas kernels: 79.2 us -> 74.8 us  [on_device(): pl.pallas_call(functools.partial(kernel, peers, dps, heads, hdim, rows),...]
    squeeze x2 -> x0, local copies, waits for them, and re-layouts: 2 us -> none  [the longest x1 1.33 us: on_device(): red[gain_rows, :heads]]
    pallas_call x0 -> x1, Pallas kernels: none -> 1.93 us  [on_device(): pl.pallas_call(hand_over, out_shape=tuple((jax.ShapeDtypeStruct(g.shape,...]
    reshape x1 -> x0, local copies, waits for them, and re-layouts: 1.29 us -> none  [on_device(): red[:gain_rows].reshape(width)]
where the time goes in v2:
time: 77.5 us; the launch traced here: 77.3 us
  Pallas kernels  76.7 us (99%)
    pallas_call x1, Pallas kernels, on_device(): pl.pallas_call(functools.partial(kernel, peers, dps, heads, hdim, rows),...  74.8 us
    pallas_call x1, Pallas kernels, on_device(): pl.pallas_call(hand_over, out_shape=tuple((jax.ShapeDtypeStruct(g.shape,...  1.93 us

profile of v2, /device:TPU:0, one launch (start us, length us, event | category | flops | bytes accessed | tf_op | source)
XLA Modules:
  0.0 77.3 jit_solution(14046492300814514769)
XLA Ops:
  0.6 74.8 %scan_layer.1 = (bf16[128,2048]{1,0:T(8,128)(2,1)}, bf16[128,128]{1,0:T(8,128)(2,1)}, bf16[128,128]{1,0:T(8,128)(2,1)}, f32[64,128]{1,0:T(8,128)}, f32[16,128]{1...) custom-call(bf16[128,2048]{1,0:T(8,128)(2,1)} %bitcast.23, bf16[128,2048]{1,0:T(8,128)(2,1)} %bitcast.24, ...), custom_call_target="tpu_custom_call" | custom-call | tf_op jit(solution)/shard_map/scan_layer/pallas_call | solution.py:421
  75.4 1.9 %hand_over.1 = (bf16[128,2048]{1,0:T(8,128)(2,1)}, bf16[128,128]{1,0:T(8,128)(2,1)}, bf16[128,128]{1,0:T(8,128)(2,1)}, f32[64,128]{1,0:T(8,128)}, f32[16,128]{1,...) custom-call(bf16[128,2048]{1,0:T(8,128)(2,1)} %get-tuple-element.21.refs_0_, bf16[128,128]{1,0:T(8,128)(2,1)} %get-tuple-element.22.refs_1_, ...), custom_call_target="tpu_custom_call" | custom-call | tf_op jit(solution)/shard_map/hand_over/pallas_call | solution.py:463

commit v3 on v2

--- a/solution.py
+++ b/solution.py
@@ -67,9 +67,18 @@
 
     barrier = pltpu.get_barrier_semaphore()
 
-    @pl.loop(1, team)
-    def _(d):
-        pl.semaphore_signal(barrier, inc=1, device_id=teammate(d), device_id_type=MESH)
+    @pl.when(jnp.logical_not(is_first))
+    def _():
+        pl.semaphore_signal(barrier, inc=1, device_id={"seq": left}, device_id_type=MESH)
+
+    @pl.when(jnp.logical_not(is_last))
+    def _():
+        pl.semaphore_signal(barrier, inc=1, device_id={"seq": right}, device_id_type=MESH)
+
+    for d in range(1, dps):
+        pl.semaphore_signal(
+            barrier, inc=1, device_id={"dp": lax.rem(mine + d, dps)}, device_id_type=MESH
+        )
 
     piece = span // PIECES
 
@@ -159,23 +168,29 @@
             parts.append(ref[:, pl.ds(at, 128)].astype(F32).T)
         return jnp.concatenate(parts, axis=0)
 
-    pl.semaphore_wait(barrier, team - 1)
-
-    def local_state(k, carry):
+    def local_state(k):
         xk = to_tokens_last(x_ref, k)
         xt[k] = xk.astype(BF16)
         high, low = split(xk * per_head(dtwoutr, k))
         hend[k] = nn(jnp.concatenate([high, low], axis=1), b_rows)
 
+    def send_local(k):
         @pl.when(is_first & (not_alone))
         def _():
             for s in range(PIECES):
                 forward_copy(k, s).start()
 
-        return carry
-
     not_alone = peers > 1
-    lax.fori_loop(0, chunks, local_state, 0)
+    local_state(0)
+    pl.semaphore_wait(
+        barrier, jnp.minimum(me, 1) + jnp.minimum(peers - 1 - me, 1) + dps - 1
+    )
+    send_local(0)
+
+    @pl.loop(1, chunks)
+    def _(k):
+        local_state(k)
+        send_local(k)
 
     @pl.when(is_first)
     def _():
@@ -292,7 +307,7 @@
             total = total + slots[d]
         return total
 
-    copy1 = exchange("seq", peers, me, part, seq_slots, r1_send, r1_recv)
+    copy1 = exchange("dp", dps, mine, part, dp_slots, r2_send, r2_recv)
 
     def backward(k, carry):
         dyk = dyt[k]
@@ -335,10 +350,10 @@
             gx_ref[:, pl.ds(at, 128)] = gx[t * 128:(t + 1) * 128].T.astype(BF16)
         return carry
 
-    lax.fori_loop(0, chunks, backward, 0)
-
-    part2[...] = collect(peers, me, seq_slots, r1_send, r1_recv, part)
-    copy2 = exchange("dp", dps, mine, part2, dp_slots, r2_send, r2_recv)
+    lax.fori_loop(0, chunks - 1, backward, 0)
+    part2[...] = collect(dps, mine, dp_slots, r2_send, r2_recv, part)
+    copy2 = exchange("seq", peers, me, part2, seq_slots, r1_send, r1_recv)
+    lax.fori_loop(chunks - 1, chunks, backward, 0)
 
     rows_of = s2[...].reshape(heads, rows)
     dcum = s1[...].reshape(heads, rows) - rows_of
@@ -366,7 +381,7 @@
     gc_ref[...] = (gcacc[...] + nn(dg_high, bs) + nn(dg_low, bs)).astype(BF16)
     gb_ref[...] = (gbacc[...] + tn(dg_high, cs) + tn(dg_low, cs)).astype(BF16)
 
-    total = collect(dps, mine, dp_slots, r2_send, r2_recv, part2)
+    total = collect(peers, me, seq_slots, r1_send, r1_recv, part2)
     gain_out[...] = total[0:gain_rows]
     skip_out[...] = total[gain_rows:gain_rows + 1, 0:heads]
     if team > 1:
@@ -378,9 +393,9 @@
             all_slots.at[pl.ds(0, team - 1)], all_slots.at[pl.ds(1, team - 1)], r3_send
         ).wait()
     alog_out[...] = jnp.sum(all_slots[...], axis=0)[:, 0:heads]
+    for d in range(1, dps):
+        copy1(d).wait_send()
     for d in range(1, peers):
-        copy1(d).wait_send()
-    for d in range(1, dps):
         copy2(d).wait_send()
 
     @pl.when(jnp.logical_not(is_last))

time: 77.5 us -> 73.3 us (0.946)
  Pallas kernels: 76.7 us -> 72.5 us
    pallas_call x1, Pallas kernels: 74.8 us -> 70.6 us  [on_device(): pl.pallas_call(functools.partial(kernel, peers, dps, heads, hdim, rows),...]
where the time goes in v3:
time: 73.3 us; the launch traced here: 73.1 us
  Pallas kernels  72.5 us (99%)
    pallas_call x1, Pallas kernels, on_device(): pl.pallas_call(functools.partial(kernel, peers, dps, heads, hdim, rows),...  70.6 us
    pallas_call x1, Pallas kernels, on_device(): pl.pallas_call(hand_over, out_shape=tuple((jax.ShapeDtypeStruct(g.shape,...  1.93 us

profile of v3, /device:TPU:0, one launch (start us, length us, event | category | flops | bytes accessed | tf_op | source)
XLA Modules:
  0.0 73.1 jit_solution(12341483661772993020)
XLA Ops:
  0.6 70.6 %scan_layer.1 = (bf16[128,2048]{1,0:T(8,128)(2,1)}, bf16[128,128]{1,0:T(8,128)(2,1)}, bf16[128,128]{1,0:T(8,128)(2,1)}, f32[64,128]{1,0:T(8,128)}, f32[16,128]{1...) custom-call(bf16[128,2048]{1,0:T(8,128)(2,1)} %bitcast.23, bf16[128,2048]{1,0:T(8,128)(2,1)} %bitcast.24, ...), custom_call_target="tpu_custom_call" | custom-call | tf_op jit(solution)/shard_map/scan_layer/pallas_call | solution.py:436
  71.2 1.9 %hand_over.1 = (bf16[128,2048]{1,0:T(8,128)(2,1)}, bf16[128,128]{1,0:T(8,128)(2,1)}, bf16[128,128]{1,0:T(8,128)(2,1)}, f32[64,128]{1,0:T(8,128)}, f32[16,128]{1,...) custom-call(bf16[128,2048]{1,0:T(8,128)(2,1)} %get-tuple-element.21.refs_0_, bf16[128,128]{1,0:T(8,128)(2,1)} %get-tuple-element.22.refs_1_, ...), custom_call_target="tpu_custom_call" | custom-call | tf_op jit(solution)/shard_map/hand_over/pallas_call | solution.py:478

commit v4 on v3

--- a/solution.py
+++ b/solution.py
@@ -39,14 +39,14 @@
 
 def kernel(
     peers, dps, heads, hdim, rows,
-    x_ref, z_ref, b_ref, c_ref, raw_ref, alog_ref, skip_ref, gain_ref, spans_ref, cot_ref,
+    x_ref, z_hbm, b_ref, c_ref, raw_ref, alog_ref, skip_ref, gain_ref, spans_ref, cot_hbm,
     gx_ref, gb_ref, gc_ref, gdt_ref, gain_out, skip_out, alog_out,
     xt, gate, dnorm, cott, gated, yns, dyt,
     hin, hend, gin, gout,
     ldt, mhigh, mlow, gmat_ref, bias_ref,
     cumr, cumc, dtr, winr, dtwoutr, skipr, ablkr, lar,
     s1, s2, sk, lastr, dgm, gcacc, gbacc, stat,
-    part, seq_slots, part2, dp_slots, part3, all_slots,
+    z_ref, cot_ref, in_sems, part, seq_slots, part2, dp_slots, part3, all_slots,
     fs_send, fs_recv, bs_send, bs_recv, r1_send, r1_recv, r2_send, r2_recv, r3_send, r3_recv,
 ):
     width = heads * hdim
@@ -61,6 +61,10 @@
     left = jnp.maximum(me - 1, 0)
 
     team = peers * dps
+    z_copy = pltpu.make_async_copy(z_hbm, z_ref, in_sems.at[0])
+    cot_copy = pltpu.make_async_copy(cot_hbm, cot_ref, in_sems.at[1])
+    z_copy.start()
+    cot_copy.start()
 
     def teammate(d):
         return {"seq": lax.rem(me + d // dps, peers), "dp": lax.rem(mine + d % dps, dps)}
@@ -245,6 +249,8 @@
         stat[1:2, :] += jnp.sum(gk * dnormk, axis=0, keepdims=True)
         return carry
 
+    z_copy.wait()
+    cot_copy.wait()
     lax.fori_loop(0, chunks, forward, 0)
 
     scale = lax.rsqrt(stat[0:1, :] / width + EPS)
@@ -428,6 +434,7 @@
     span = GROUP * hdim
     red_rows = width // 128 + 8
     vmem = pl.BlockSpec(memory_space=pltpu.VMEM)
+    anywhere = pl.BlockSpec(memory_space=pl.ANY)
     wide = lambda dtype=F32: pltpu.VMEM((chunks, span, rows), dtype)
     states = pltpu.VMEM((chunks, span, state), F32)
     small = pltpu.VMEM((chunks, GROUP, rows), F32)
@@ -444,7 +451,7 @@
             jax.ShapeDtypeStruct((1, heads), F32),
             jax.ShapeDtypeStruct((1, heads), F32),
         ),
-        in_specs=[vmem] * 8 + [pl.BlockSpec(memory_space=pltpu.SMEM), vmem],
+        in_specs=[vmem, anywhere] + [vmem] * 6 + [pl.BlockSpec(memory_space=pltpu.SMEM), anywhere],
         out_specs=(vmem,) * 7,
         scratch_shapes=[
             wide(BF16), wide(), wide(), wide(), wide(), wide(), wide(),
@@ -458,6 +465,7 @@
             small, small, small, small,
             square, pltpu.VMEM((rows, state), F32), pltpu.VMEM((rows, state), F32),
             pltpu.VMEM((8, rows), F32),
+            pltpu.VMEM((rows, width), BF16), pltpu.VMEM((rows, width), BF16), pltpu.SemaphoreType.DMA((2,)),
             pltpu.VMEM((red_rows, 128), F32),
             pltpu.VMEM((peers, red_rows, 128), F32),
             pltpu.VMEM((red_rows, 128), F32),

time: 73.3 us -> 73.1 us (level)
  no operation moved by 1% of the time
where the time goes in v4:
time: 73.1 us; the launch traced here: 72.9 us
  Pallas kernels  72.2 us (99%)
    pallas_call x1, Pallas kernels, on_device(): pl.pallas_call(functools.partial(kernel, peers, dps, heads, hdim, rows),...  70.3 us
    pallas_call x1, Pallas kernels, on_device(): pl.pallas_call(hand_over, out_shape=tuple((jax.ShapeDtypeStruct(g.shape,...  1.93 us

profile of v4, /device:TPU:0, one launch (start us, length us, event | category | flops | bytes accessed | tf_op | source)
XLA Modules:
  0.0 72.9 jit_solution(638192670804835847)
XLA Ops:
  0.6 70.3 %scan_layer.1 = (bf16[128,2048]{1,0:T(8,128)(2,1)}, bf16[128,128]{1,0:T(8,128)(2,1)}, bf16[128,128]{1,0:T(8,128)(2,1)}, f32[64,128]{1,0:T(8,128)}, f32[16,128]{1...) custom-call(bf16[128,2048]{1,0:T(8,128)(2,1)} %bitcast.23, bf16[128,2048]{1,0:T(8,128)(2,1)} %bitcast.24, ...), custom_call_target="tpu_custom_call" | custom-call | tf_op jit(solution)/shard_map/scan_layer/pallas_call | solution.py:443
  71.0 1.9 %hand_over.1 = (bf16[128,2048]{1,0:T(8,128)(2,1)}, bf16[128,128]{1,0:T(8,128)(2,1)}, bf16[128,128]{1,0:T(8,128)(2,1)}, f32[64,128]{1,0:T(8,128)}, f32[16,128]{1,...) custom-call(bf16[128,2048]{1,0:T(8,128)(2,1)} %get-tuple-element.21.refs_0_, bf16[128,128]{1,0:T(8,128)(2,1)} %get-tuple-element.22.refs_1_, ...), custom_call_target="tpu_custom_call" | custom-call | tf_op jit(solution)/shard_map/hand_over/pallas_call | solution.py:486
